TPU v7x, 32 devices: a whole 2x2x4 slice. The times are simulated.
32 devices in a mesh: pair: 8 (over z, y), band: 4 (over x, core).
Axes of the slice: x: 2, y: 2, z: 4, core: 2. Of those that a mesh axis runs over, the one named last changes fastest.
Arguments:
- orbitals: bfloat16 [2048, 23, 64], P('pair'), may hold values from -6 to 6
- screening: bfloat16 [1024, 8, 1024], P('pair', None, 'band'), may hold values from -0.1875 to 0.1875
- trial: bfloat16 [1024, 23, 64], P('pair'), may hold values from -6 to 6
- pair_kpts: int32 [8, 2], replicated, may hold values from 0 to 22
- pair_q: int32 [8], replicated, may hold values from 0 to 7
Outputs:
- applied: float32 [1024, 23, 64], P('pair', None, 'band')
All inputs are finite; a program needn't handle non-finite values.
Results may differ from a plain program's by a relative error of at most 0.013.
Values may be sent and summed in bfloat16 or wider, within the bound.
No kernel may reach another device: no remote copies, remote signals or barrier semaphores. Data moves between devices by JAX's collectives and lax.ppermute only.
A program may use at most 64 MiB of HBM per device.

v0:
```python
import math
import jax
import jax.numpy as jnp
from jax import lax
from jax.sharding import PartitionSpec as P

NV = 32
NC = 32
NR = 2048
NG = 1024
KPTS = 23
NB = 64


def basis_rows(first_row, row_count, point_count):
    frequency = first_row + jnp.arange(row_count, dtype=jnp.int32)
    position = jnp.arange(point_count, dtype=jnp.int32)
    phase_index = (2 * position[None, :] + 1) * frequency[:, None] % (4 * point_count)
    values = jnp.cos(phase_index.astype(jnp.float32) * (math.pi / (2 * point_count))) * math.sqrt(
        2.0 / point_count
    )
    return values.astype(jnp.bfloat16)


def densities(first_set, second_set):
    merged = first_set.astype(jnp.float32)[:, :, None] * second_set.astype(jnp.float32)[:, None, :]
    return merged.reshape(first_set.shape[0], first_set.shape[1] * second_set.shape[1]).astype(
        jnp.bfloat16
    )


def transform(basis_block, first_set, second_set):
    return lax.dot_general(
        basis_block,
        densities(first_set, second_set),
        (((1,), (0,)), ((), ())),
        preferred_element_type=jnp.float32,
    ).astype(jnp.bfloat16)


def on_device(orbitals, screening, trial, pair_kpts, pair_q):
    band_count = lax.axis_size("band")
    pair_count = lax.axis_size("pair")
    pair_here = lax.axis_index("pair")
    own_kpts = lax.dynamic_index_in_dim(pair_kpts, pair_here, 0, keepdims=False)
    listed = pair_kpts.shape[0]
    vector_count = trial.shape[2]
    orbital_send = orbitals[:, pair_kpts].reshape(orbitals.shape[0], listed, 2 * NB)
    trial_send = trial[:, pair_kpts].reshape(trial.shape[0], listed, 2 * vector_count)
    screen_send = screening[:, pair_q]
    orbital_got, trial_got, screen_got = (
        lax.all_to_all(orbital_send, "pair", split_axis=1, concat_axis=0, tiled=True),
        lax.all_to_all(trial_send, "pair", split_axis=1, concat_axis=0, tiled=True),
        lax.all_to_all(screen_send, "pair", split_axis=1, concat_axis=0, tiled=True),
    )
    screen_cols = screen_got[:, 0]
    first_orb = orbital_got[:, 0, :NB]
    second_orb = orbital_got[:, 0, NB:]
    row_count = NG // band_count
    basis_block = basis_rows(lax.axis_index("band") * row_count, row_count, NR)
    valence = transform(basis_block, first_orb[:, :NV], second_orb[:, :NV])
    conduction = transform(basis_block, first_orb[:, NV:], second_orb[:, NV:])
    screened = lax.dot_general(
        screen_cols,
        lax.all_gather(valence, "band", axis=0, tiled=True),
        (((0,), (0,)), ((), ())),
        preferred_element_type=jnp.float32,
    ).astype(jnp.bfloat16)
    raw = lax.dot_general(
        conduction, screened, (((0,), (0,)), ((), ())), preferred_element_type=jnp.float32
    ) * (1.0 / math.sqrt(NG))
    kernel = (
        raw.reshape(NC, NC, NV, NV)
        .transpose(2, 0, 3, 1)
        .reshape(NV * NC, NV * NC)
        .astype(jnp.bfloat16)
    )
    trial_first = trial_got[:, 0, :vector_count]
    trial_second = trial_got[:, 0, vector_count:]
    apply_scale = 1.0 / math.sqrt(NV * NC)
    forward = (
        lax.dot_general(
            kernel, trial_second, (((1,), (0,)), ((), ())), preferred_element_type=jnp.float32
        )
        * apply_scale
    )
    backward = (
        lax.dot_general(
            kernel, trial_first, (((0,), (0,)), ((), ())), preferred_element_type=jnp.float32
        )
        * apply_scale
    )
    partials = jnp.stack([forward, backward])
    summed = lax.psum_scatter(
        partials.astype(jnp.bfloat16), "band", scatter_dimension=2, tiled=True
    ).astype(jnp.float32)
    share = summed.shape[2]
    state_rows = summed.shape[1] // pair_count
    kpt_ids = jnp.arange(KPTS, dtype=jnp.int32)
    one_hot = (own_kpts[:, None] == kpt_ids[None, :]).astype(jnp.float32)
    spread = (
        summed[0][:, None, :] * one_hot[0][None, :, None]
        + summed[1][:, None, :] * one_hot[1][None, :, None]
    )
    spread = spread.reshape(summed.shape[1], KPTS * share)
    scattered = lax.psum_scatter(spread, "pair", scatter_dimension=0, tiled=True)
    return scattered.reshape(state_rows, KPTS, share)


def solution(mesh):
    return jax.shard_map(
        on_device,
        mesh=mesh,
        in_specs=(P("pair", None, None), P("pair", None, "band"), P("pair", None, None), P(), P()),
        out_specs=P("pair", None, "band"),
        check_vma=False,
    )
```

profile of v0, /device:TPU:0, one launch (start us, length us, event | category | flops | bytes accessed | tf_op | source)
XLA Modules:
  0.0 212.1 jit_solution(7176523066295668518)
XLA Ops:
  6.5 0.8 compare_select_fusion
  7.5 0.2 copy-done
  7.7 1.4 gather_fusion
  9.1 7.3 %all-to-all-start = ((bf16[256,8,128]{0,2,1:T(8,128)(2,1)}), bf16[256,8,128]{0,2,1:T(8,128)(2,1)S(1)}, u32[]{:S(2)}, u32[]{:S(2)}) async-start(bf16[256,8,128]{0,2,1:T(8,128)(2,1)} %bitcast.2), calls=%async_computation | async-start | bytes 1048576 | tf_op jit(solution)/shard_map/all_to_all | solution.py:52
  16.4 14.4 %all-to-all-done = bf16[256,8,128]{0,2,1:T(8,128)(2,1)S(1)} async-done(((bf16[256,8,128]{0,2,1:T(8,128)(2,1)}), bf16[256,8,128]{0,2,1:T(8,128)(2,1)S(1)}, u32[]{:S(2)}, u32[]{:S(2)}) %all-to-all-start) | async-done | bytes 524320 | tf_op jit(solution)/shard_map/all_to_all | solution.py:52
  30.9 0.3 copy.26
  31.1 0.2 fusion.23
  31.3 0.2 copy.28
  31.6 0.2 copy.27
  31.8 4.2 %multiply_convert_fusion = (bf16[2048,32,32]{0,2,1:T(8,128)(2,1)S(1)}, bf16[2048,32,32]{0,2,1:T(8,128)(2,1)}) fusion(f32[2048,32]{0,1:T(8,128)S(1)} %get-tuple-element.9, f32[2048,32]{0,1:T(8,128)S(1)} %get-tuple-element.7, f32[2048,32]{0,1:T(8,128)S(1)} %get-tuple-element.10, f32[2048,32]{0,1:T(8,128)S(1)} %get-tuple-element.8), kind=kLoop, calls=%fused_computation.3 | loop fusion | flops 8388608 | bytes 9437184 | tf_op jit(solution)/shard_map/convert_element_type | solution.py:27
  36.0 10.2 %convolution_convert_fusion.1 = bf16[256,1024]{1,0:T(8,128)(2,1)} fusion(bf16[2048,1024]{0,1:T(8,128)(2,1)S(1)} %bitcast.70, s32[256]{0:T(256)S(1)} %iota_add_fusion, s32[2048]{0:T(1024)S(1)} %multiply_add_fusion), kind=kOutput, calls=%fused_computation.21 | convolution fusion | flops 1082392576 | bytes 4727808 | tf_op jit(solution)/shard_map/dot_general | solution.py:33
  46.3 1.3 gather_fusion.2
  47.6 3.6 %all-to-all-start.2 = ((bf16[128,8,128]{0,2,1:T(8,128)(2,1)}), bf16[128,8,128]{0,2,1:T(8,128)(2,1)S(1)}, u32[]{:S(2)}, u32[]{:S(2)}) async-start(bf16[128,8,128]{0,2,1:T(8,128)(2,1)} %bitcast.17), calls=%async_computation.2 | async-start | bytes 524288 | tf_op jit(solution)/shard_map/all_to_all | solution.py:53
  51.3 2.0 gather_fusion.1
  53.3 0.9 copy.29
  54.2 6.1 %all-to-all-done.2 = bf16[128,8,128]{0,2,1:T(8,128)(2,1)S(1)} async-done(((bf16[128,8,128]{0,2,1:T(8,128)(2,1)}), bf16[128,8,128]{0,2,1:T(8,128)(2,1)S(1)}, u32[]{:S(2)}, u32[]{:S(2)}) %all-to-all-start.2) | async-done | bytes 262176 | tf_op jit(solution)/shard_map/all_to_all | solution.py:53
  60.3 3.6 %all-to-all-start.1 = ((bf16[128,8,256]{2,0,1:T(8,128)(2,1)}), bf16[128,8,256]{2,0,1:T(8,128)(2,1)S(1)}, u32[]{:S(2)}, u32[]{:S(2)}) async-start(bf16[128,8,256]{2,0,1:T(8,128)(2,1)} %copy.29), calls=%async_computation.1 | async-start | bytes 1048576 | tf_op jit(solution)/shard_map/all_to_all | solution.py:54
  63.9 0.2 reduce-scatter.3.cloned.1.call-start
  64.3 11.5 %convolution_convert_fusion.2 = bf16[256,1024]{1,0:T(8,128)(2,1)} fusion(bf16[2048,1024]{0,1:T(8,128)(2,1)} %bitcast.69, s32[256]{0:T(256)S(1)} %iota_add_fusion, s32[2048]{0:T(1024)S(1)} %multiply_add_fusion), kind=kOutput, calls=%fused_computation.22 | convolution fusion | flops 1082392576 | bytes 4727808 | tf_op jit(solution)/shard_map/dot_general | solution.py:33
  75.8 2.3 %all-to-all-done.1 = bf16[128,8,256]{2,0,1:T(8,128)(2,1)S(1)} async-done(((bf16[128,8,256]{2,0,1:T(8,128)(2,1)}), bf16[128,8,256]{2,0,1:T(8,128)(2,1)S(1)}, u32[]{:S(2)}, u32[]{:S(2)}) %all-to-all-start.1) | async-done | bytes 524320 | tf_op jit(solution)/shard_map/all_to_all | solution.py:54
  78.1 0.8 copy-done.3
  78.9 3.3 %multiply_convert_fusion.2 = bf16[1024,1024]{1,0:T(8,128)(2,1)S(1)} fusion(bf16[256,1024]{1,0:T(8,128)(2,1)} %convolution_convert_fusion.2, bf16[1024,256]{1,0:T(8,128)(2,1)} %bitcast.78, bf16[1024,1024]{1,0:T(8,128)(2,1)} %all-gather.2.cloned.1.call-done), kind=kOutput, calls=%fused_computation.5 | convolution fusion | flops 1076101120 | bytes 5242880 | tf_op jit(solution)/shard_map/dot_general | solution.py:69
  82.2 8.2 %convert_element_type.73 = bf16[32,32,32,32]{3,2,1,0:T(8,128)(2,1)} reshape(bf16[1024,1024]{1,0:T(8,128)(2,1)S(1)} %multiply_convert_fusion.2) | data formatting | bytes 4194304 | tf_op jit(solution)/shard_map/convert_element_type | solution.py:76
  90.4 15.2 %copy.30 = bf16[32,32,32,32]{1,3,0,2:T(8,128)(2,1)} copy(bf16[32,32,32,32]{3,2,1,0:T(8,128)(2,1)} %convert_element_type.73) | data formatting | bytes 4194304 | tf_op jit(solution)/shard_map/convert_element_type | solution.py:76
  105.6 11.3 %convert_element_type.75 = bf16[1024,1024]{1,0:T(8,128)(2,1)S(1)} reshape(bf16[32,32,32,32]{3,2,1,0:T(8,128)(2,1)} %bitcast.67) | data formatting | bytes 4194304 | tf_op jit(solution)/shard_map/convert_element_type | solution.py:76
  116.9 0.8 fusion.10
  117.8 0.5 fusion.9
  118.3 0.7 pad_maximum_fusion
  119.7 18.6 %reduce-scatter.3.cloned.1.call-done = bf16[2,1024,16]{1,2,0:T(8,128)(2,1)} async-done(((bf16[2,1024,64]{1,2,0:T(8,128)(2,1)}), bf16[2,1024,16]{1,2,0:T(8,128)(2,1)}) %reduce-scatter.3.cloned.1.call-update) | async-done | bytes 65552 | tf_op jit(solution)/shard_map/reduce_scatter | solution.py:94
  138.3 0.8 convert_element_type.76
  139.2 1.4 fusion.6
  140.6 65.0 %reduce-scatter.5.cloned.1.call-done = f32[128,368]{0,1:T(8,128)} async-done(((f32[1024,368]{0,1:T(8,128)}), f32[128,368]{0,1:T(8,128)}) %reduce-scatter.5.cloned.1.call-update) | async-done | bytes 188432 | tf_op jit(solution)/shard_map/reduce_scatter | solution.py:106
  (34 shorter events, 1.2 us)
Async XLA Ops:
  6.5 1.1 copy-start
  9.1 21.8 %all-to-all-start = ((bf16[256,8,128]{0,2,1:T(8,128)(2,1)}), bf16[256,8,128]{0,2,1:T(8,128)(2,1)S(1)}, u32[]{:S(2)}, u32[]{:S(2)}) async-start(bf16[256,8,128]{0,2,1:T(8,128)(2,1)} %bitcast.2), calls=%async_computation | async-start | bytes 1048576 | tf_op jit(solution)/shard_map/all_to_all | solution.py:52
  16.4 61.8 %all-gather.2.cloned.1.call-start = ((), (), s32[]{:S(2)}) async-start(), calls=%async_computation.5 | async-start | bytes 2621440 | tf_op jit(solution)/shard_map/all_gather | solution.py:65
  36.0 10.2 %copy-start.2 = (bf16[128,23,64]{0,2,1:T(8,128)(2,1)S(1)}, bf16[128,23,64]{0,2,1:T(8,128)(2,1)}, u32[]{:S(2)}) copy-start(bf16[128,23,64]{0,2,1:T(8,128)(2,1)} %param.7) | copy-start | bytes 1130500
  46.2 5.0 %copy-start.5 = (s32[8]{0:T(128)S(1)}, s32[8]{0:T(128)}, u32[]{:S(2)}) copy-start(s32[8]{0:T(128)} %param.9) | copy-start | bytes 100
  46.2 5.0 %copy-start.1 = (bf16[128,8,256]{2,1,0:T(8,128)(2,1)S(1)}, bf16[128,8,256]{2,1,0:T(8,128)(2,1)}, u32[]{:S(2)}) copy-start(bf16[128,8,256]{2,1,0:T(8,128)(2,1)} %param.6) | copy-start | bytes 1572868
  47.6 12.7 %all-to-all-start.2 = ((bf16[128,8,128]{0,2,1:T(8,128)(2,1)}), bf16[128,8,128]{0,2,1:T(8,128)(2,1)S(1)}, u32[]{:S(2)}, u32[]{:S(2)}) async-start(bf16[128,8,128]{0,2,1:T(8,128)(2,1)} %bitcast.17), calls=%async_computation.2 | async-start | bytes 524288 | tf_op jit(solution)/shard_map/all_to_all | solution.py:53
  60.3 17.8 %all-to-all-start.1 = ((bf16[128,8,256]{2,0,1:T(8,128)(2,1)}), bf16[128,8,256]{2,0,1:T(8,128)(2,1)S(1)}, u32[]{:S(2)}, u32[]{:S(2)}) async-start(bf16[128,8,256]{2,0,1:T(8,128)(2,1)} %copy.29), calls=%async_computation.1 | async-start | bytes 1048576 | tf_op jit(solution)/shard_map/all_to_all | solution.py:54
  63.9 74.4 %reduce-scatter.3.cloned.1.call-start = ((), (), s32[]{:S(2)}) async-start(), calls=%async_computation.6 | async-start | bytes 327680 | tf_op jit(solution)/shard_map/reduce_scatter | solution.py:94
  78.1 0.8 copy-start.3
  117.7 1.3 copy-start.4
  119.0 86.5 %reduce-scatter.5.cloned.1.call-start = ((), (), s32[]{:S(2)}) async-start(), calls=%async_computation.7 | async-start | bytes 1695744 | tf_op jit(solution)/shard_map/reduce_scatter | solution.py:106
Sparse Core Ops, SparseCore 0:
  46.4 21.6 all-gather.1
  119.1 19.1 reduce-scatter.2
  141.7 63.7 reduce-scatter.4
where the time goes:
time: 213 us; the launch traced here: 212 us
  waiting for transfers between devices  106 us (50%)
  local copies, waits for them, and re-layouts  43.1 us (20%)
  matrix products  26.3 us (12%)
  starting transfers between devices  14.8 us (7%)
  between operations  13.3 us (6%)
  other arithmetic  8.09 us (4%)
    reduce_scatter x1, waiting for transfers between devices, on_device(): lax.psum_scatter(spread, 'pair', scatter_dimension=0, tiled=True)  65 us
    convert_element_type x3, local copies, waits for them, and re-layouts, on_device(): kernel = raw.reshape(NC, NC, NV, NV).transpose(2, 0, 3, 1).reshape(NV * N...  34.7 us
    dot_general x2, matrix products, transform(): lax.dot_general(basis_block, densities(first_set, second_set), (((1,), (0...  21.7 us
    reduce_scatter x1, waiting for transfers between devices, on_device(): lax.psum_scatter(partials.astype(jnp.bfloat16), 'band', scatter_dimension...  18.6 us
    all_to_all x1, waiting for transfers between devices, on_device(): lax.all_to_all(orbital_send, 'pair', split_axis=1, concat_axis=0, tiled=T...  14.4 us
    all_to_all x1, starting transfers between devices, on_device(): lax.all_to_all(orbital_send, 'pair', split_axis=1, concat_axis=0, tiled=T...  7.31 us
    all_to_all x1, waiting for transfers between devices, on_device(): lax.all_to_all(trial_send, 'pair', split_axis=1, concat_axis=0, tiled=True)  6.1 us
  transfers between devices with their start and end apart: 6, of which 5 were waited for; matrix products, arithmetic and copies ran while one was open for 8% of the time, Pallas kernels for 0%

commit v1 on v0

--- a/solution.py
+++ b/solution.py
@@ -10,6 +10,18 @@
 NG = 1024
 KPTS = 23
 NB = 64
+
+
+def rotated_exchange(x, axis, split, join):
+    ways, here = (lax.axis_size(axis), lax.axis_index(axis))
+    width = x.shape[split] // ways
+    turned = jnp.roll(x, -here * width, axis=split)
+    got = [lax.slice_in_dim(turned, 0, width, axis=split)]
+    for far in range(1, ways):
+        sent = lax.slice_in_dim(turned, far * width, (far + 1) * width, axis=split)
+        got.append(lax.ppermute(sent, axis, [(d, (d + far) % ways) for d in range(ways)]))
+    line = jnp.concatenate(got[::-1], axis=join)
+    return jnp.roll(line, (here + 1) * got[0].shape[join], axis=join)
 
 
 def basis_rows(first_row, row_count, point_count):
@@ -49,7 +61,7 @@
     trial_send = trial[:, pair_kpts].reshape(trial.shape[0], listed, 2 * vector_count)
     screen_send = screening[:, pair_q]
     orbital_got, trial_got, screen_got = (
-        lax.all_to_all(orbital_send, "pair", split_axis=1, concat_axis=0, tiled=True),
+        rotated_exchange(orbital_send, "pair", 1, 0),
         lax.all_to_all(trial_send, "pair", split_axis=1, concat_axis=0, tiled=True),
         lax.all_to_all(screen_send, "pair", split_axis=1, concat_axis=0, tiled=True),
     )

time: 213 us -> 206 us (0.967)
  waiting for transfers between devices: 106 us -> 98.5 us
  starting transfers between devices: 14.8 us -> 19.8 us
    all_to_all x1 -> x0, waiting for transfers between devices: 14.4 us -> none  [on_device(): lax.all_to_all(orbital_send, 'pair', split_axis=1, concat_axis=0, tiled=T...]
    ppermute x0 -> x7, starting transfers between devices: none -> 12.6 us  [rotated_exchange(): lax.ppermute(sent, axis, [(d, (d + far) % ways) for d in range(ways)])]
    ppermute x0 -> x7, waiting for transfers between devices: none -> 7.49 us  [rotated_exchange(): lax.ppermute(sent, axis, [(d, (d + far) % ways) for d in range(ways)])]
    all_to_all x1 -> x0, starting transfers between devices: 7.31 us -> none  [on_device(): lax.all_to_all(orbital_send, 'pair', split_axis=1, concat_axis=0, tiled=T...]
  transfers between devices with their start and end apart: 6 -> 12, of which waited for: 5 -> 6; matrix products, arithmetic and copies ran while one was open for 8% -> 8% of each run, Pallas kernels for 0% -> 0%
where the time goes in v1:
time: 206 us; the launch traced here: 205 us
  waiting for transfers between devices  98.5 us (48%)
  local copies, waits for them, and re-layouts  41.1 us (20%)
  matrix products  25.1 us (12%)
  starting transfers between devices  19.8 us (10%)
  between operations  13.4 us (7%)
  other arithmetic  6.91 us (3%)
    reduce_scatter x1, waiting for transfers between devices, on_device(): lax.psum_scatter(spread, 'pair', scatter_dimension=0, tiled=True)  65 us
    convert_element_type x3, local copies, waits for them, and re-layouts, on_device(): kernel = raw.reshape(NC, NC, NV, NV).transpose(2, 0, 3, 1).reshape(NV * N...  34.5 us
    dot_general x2, matrix products, transform(): lax.dot_general(basis_block, densities(first_set, second_set), (((1,), (0...  20.4 us
    reduce_scatter x1, waiting for transfers between devices, on_device(): lax.psum_scatter(partials.astype(jnp.bfloat16), 'band', scatter_dimension...  18.7 us
    ppermute x7, starting transfers between devices, rotated_exchange(): lax.ppermute(sent, axis, [(d, (d + far) % ways) for d in range(ways)])  12.6 us
    ppermute x7, waiting for transfers between devices, rotated_exchange(): lax.ppermute(sent, axis, [(d, (d + far) % ways) for d in range(ways)])  7.49 us
    all_to_all x1, waiting for transfers between devices, on_device(): lax.all_to_all(trial_send, 'pair', split_axis=1, concat_axis=0, tiled=True)  5.21 us
  transfers between devices with their start and end apart: 12, of which 6 were waited for; matrix products, arithmetic and copies ran while one was open for 8% of the time, Pallas kernels for 0%

profile of v1, /device:TPU:0, one launch (start us, length us, event | category | flops | bytes accessed | tf_op | source)
XLA Modules:
  0.0 204.8 jit_solution(17450906032185378614)
XLA Ops:
  6.5 0.8 compare_select_fusion
  7.5 0.7 compare_select_fusion.1
  8.1 0.6 gather_fusion
  9.0 6.1 %collective-permute-start = (bf16[256,1,128]{0,2,1:T(8,128)(2,1)S(1)}, bf16[256,1,128]{0,2,1:T(8,128)(2,1)S(1)}, u32[]{:S(2)}, u32[]{:S(2)}) collective-permute-start(bf16[256,1,128]{0,2,1:T(8,128)(2,1)S(1)} %get-tuple-element.13), channel_id=1, source_target_pairs={{0,28},{4,0},{8,4},{12,8},{16,12},{20,16},{24,20},{28,24},{1,29},{... | collective-permute-start | bytes 196616 | tf_op jit(solution)/shard_map/ppermute | solution.py:22
  15.5 3.0 %collective-permute-start.3 = (bf16[256,1,128]{0,2,1:T(8,128)(2,1)S(1)}, bf16[256,1,128]{0,2,1:T(8,128)(2,1)S(1)}, u32[]{:S(2)}, u32[]{:S(2)}) collective-permute-start(bf16[256,1,128]{0,2,1:T(8,128)(2,1)S(1)} %get-tuple-element.10), channel_id=1, source_target_pairs={{0,16},{4,20},{8,24},{12,28},{16,0},{20,4},{24,8},{28,12},{1,17},{... | collective-permute-start | bytes 196616 | tf_op jit(solution)/shard_map/ppermute | solution.py:22
  18.5 1.9 collective-permute-start.5
  20.4 1.2 collective-permute-start.6
  21.6 4.8 %collective-permute-done.3 = bf16[256,1,128]{0,2,1:T(8,128)(2,1)S(1)} collective-permute-done((bf16[256,1,128]{0,2,1:T(8,128)(2,1)S(1)}, bf16[256,1,128]{0,2,1:T(8,128)(2,1)S(1)}, u32[]{:S(2)}, u32[]{:S(2)}) %collective-permute-start.3) | collective-permute-done | bytes 65568 | tf_op jit(solution)/shard_map/ppermute | solution.py:22
  26.4 2.7 %collective-permute-done.4 = bf16[256,1,128]{0,2,1:T(8,128)(2,1)S(1)} collective-permute-done((bf16[256,1,128]{0,2,1:T(8,128)(2,1)S(1)}, bf16[256,1,128]{0,2,1:T(8,128)(2,1)S(1)}, u32[]{:S(2)}, u32[]{:S(2)}) %collective-permute-start.4) | collective-permute-done | bytes 65568 | tf_op jit(solution)/shard_map/ppermute | solution.py:22
  29.5 1.1 multiply_convert_fusion
  30.6 10.2 %convolution_convert_fusion.1 = bf16[256,1024]{1,0:T(8,128)(2,1)} fusion(bf16[2048,1024]{0,1:T(8,128)(2,1)S(1)} %bitcast.68, s32[256]{0:T(256)S(1)} %iota_add_fusion, s32[2048]{0:T(1024)S(1)} %multiply_add_fusion), kind=kOutput, calls=%fused_computation.21 | convolution fusion | flops 1082392576 | bytes 4727808 | tf_op jit(solution)/shard_map/dot_general | solution.py:45
  40.8 1.3 gather_fusion.2
  42.1 3.4 %all-to-all-start.1 = ((bf16[128,8,128]{0,2,1:T(8,128)(2,1)}), bf16[128,8,128]{0,2,1:T(8,128)(2,1)S(1)}, u32[]{:S(2)}, u32[]{:S(2)}) async-start(bf16[128,8,128]{0,2,1:T(8,128)(2,1)} %bitcast.14), calls=%async_computation.1 | async-start | bytes 524288 | tf_op jit(solution)/shard_map/all_to_all | solution.py:65
  45.5 2.0 gather_fusion.1
  47.6 0.9 copy.24
  48.5 5.2 %all-to-all-done.1 = bf16[128,8,128]{0,2,1:T(8,128)(2,1)S(1)} async-done(((bf16[128,8,128]{0,2,1:T(8,128)(2,1)}), bf16[128,8,128]{0,2,1:T(8,128)(2,1)S(1)}, u32[]{:S(2)}, u32[]{:S(2)}) %all-to-all-start.1) | async-done | bytes 262176 | tf_op jit(solution)/shard_map/all_to_all | solution.py:65
  53.7 3.5 %all-to-all-start = ((bf16[128,8,256]{2,0,1:T(8,128)(2,1)}), bf16[128,8,256]{2,0,1:T(8,128)(2,1)S(1)}, u32[]{:S(2)}, u32[]{:S(2)}) async-start(bf16[128,8,256]{2,0,1:T(8,128)(2,1)} %copy.24), calls=%async_computation | async-start | bytes 1048576 | tf_op jit(solution)/shard_map/all_to_all | solution.py:66
  57.4 1.1 multiply_convert_fusion.1
  58.5 10.2 %convolution_convert_fusion.2 = bf16[256,1024]{1,0:T(8,128)(2,1)} fusion(bf16[2048,1024]{0,1:T(8,128)(2,1)S(1)} %bitcast.67, s32[256]{0:T(256)S(1)} %iota_add_fusion, s32[2048]{0:T(1024)S(1)} %multiply_add_fusion), kind=kOutput, calls=%fused_computation.22 | convolution fusion | flops 1082392576 | bytes 4727808 | tf_op jit(solution)/shard_map/dot_general | solution.py:45
  68.9 2.0 all-to-all-done
  70.9 0.8 copy-done.3
  71.7 3.3 %multiply_convert_fusion.2 = bf16[1024,1024]{1,0:T(8,128)(2,1)S(1)} fusion(bf16[256,1024]{1,0:T(8,128)(2,1)} %convolution_convert_fusion.2, bf16[1024,256]{1,0:T(8,128)(2,1)} %bitcast.73, bf16[1024,1024]{1,0:T(8,128)(2,1)} %all-gather.2.cloned.1.call-done), kind=kOutput, calls=%fused_computation.5 | convolution fusion | flops 1076101120 | bytes 5242880 | tf_op jit(solution)/shard_map/dot_general | solution.py:81
  75.0 7.9 %convert_element_type.73 = bf16[32,32,32,32]{3,2,1,0:T(8,128)(2,1)} reshape(bf16[1024,1024]{1,0:T(8,128)(2,1)S(1)} %multiply_convert_fusion.2) | data formatting | bytes 4194304 | tf_op jit(solution)/shard_map/convert_element_type | solution.py:88
  82.9 15.2 %copy.25 = bf16[32,32,32,32]{1,3,0,2:T(8,128)(2,1)} copy(bf16[32,32,32,32]{3,2,1,0:T(8,128)(2,1)} %convert_element_type.73) | data formatting | bytes 4194304 | tf_op jit(solution)/shard_map/convert_element_type | solution.py:88
  98.1 11.3 %convert_element_type.75 = bf16[1024,1024]{1,0:T(8,128)(2,1)S(1)} reshape(bf16[32,32,32,32]{3,2,1,0:T(8,128)(2,1)} %bitcast.65) | data formatting | bytes 4194304 | tf_op jit(solution)/shard_map/convert_element_type | solution.py:88
  109.4 0.8 fusion.10
  110.3 0.5 fusion.9
  110.8 0.7 pad_maximum_fusion
  112.2 18.7 %reduce-scatter.3.cloned.1.call-done = bf16[2,1024,16]{1,2,0:T(8,128)(2,1)} async-done(((bf16[2,1024,64]{1,2,0:T(8,128)(2,1)}), bf16[2,1024,16]{1,2,0:T(8,128)(2,1)}) %reduce-scatter.3.cloned.1.call-update) | async-done | bytes 65552 | tf_op jit(solution)/shard_map/reduce_scatter | solution.py:106
  130.9 0.8 convert_element_type.76
  131.8 1.4 fusion.6
  133.2 65.0 %reduce-scatter.5.cloned.1.call-done = f32[128,368]{0,1:T(8,128)} async-done(((f32[1024,368]{0,1:T(8,128)}), f32[128,368]{0,1:T(8,128)}) %reduce-scatter.5.cloned.1.call-update) | async-done | bytes 188432 | tf_op jit(solution)/shard_map/reduce_scatter | solution.py:118
  (59 shorter events, 2.2 us)
Async XLA Ops:
  6.5 1.6 copy-start
  6.5 64.4 %all-gather.2.cloned.1.call-start = ((), (), s32[]{:S(2)}) async-start(), calls=%async_computation.4 | async-start | bytes 2621440 | tf_op jit(solution)/shard_map/all_gather | solution.py:77
  9.0 9.5 %collective-permute-start = (bf16[256,1,128]{0,2,1:T(8,128)(2,1)S(1)}, bf16[256,1,128]{0,2,1:T(8,128)(2,1)S(1)}, u32[]{:S(2)}, u32[]{:S(2)}) collective-permute-start(bf16[256,1,128]{0,2,1:T(8,128)(2,1)S(1)} %get-tuple-element.13), channel_id=1, source_target_pairs={{0,28},{4,0},{8,4},{12,8},{16,12},{20,16},{24,20},{28,24},{1,29},{... | collective-permute-start | bytes 196616 | tf_op jit(solution)/shard_map/ppermute | solution.py:22
  15.1 5.4 %collective-permute-start.1 = (bf16[256,1,128]{0,2,1:T(8,128)(2,1)S(1)}, bf16[256,1,128]{0,2,1:T(8,128)(2,1)S(1)}, u32[]{:S(2)}, u32[]{:S(2)}) collective-permute-start(bf16[256,1,128]{0,2,1:T(8,128)(2,1)S(1)} %get-tuple-element.12), channel_id=1, source_target_pairs={{0,24},{4,28},{8,0},{12,4},{16,8},{20,12},{24,16},{28,20},{1,25},{... | collective-permute-start | bytes 196616 | tf_op jit(solution)/shard_map/ppermute | solution.py:22
  15.5 6.1 %collective-permute-start.2 = (bf16[256,1,128]{0,2,1:T(8,128)(2,1)S(1)}, bf16[256,1,128]{0,2,1:T(8,128)(2,1)S(1)}, u32[]{:S(2)}, u32[]{:S(2)}) collective-permute-start(bf16[256,1,128]{0,2,1:T(8,128)(2,1)S(1)} %get-tuple-element.11), channel_id=1, source_target_pairs={{0,20},{4,24},{8,28},{12,0},{16,4},{20,8},{24,12},{28,16},{1,21},{... | collective-permute-start | bytes 196616 | tf_op jit(solution)/shard_map/ppermute | solution.py:22
  15.5 10.9 %collective-permute-start.3 = (bf16[256,1,128]{0,2,1:T(8,128)(2,1)S(1)}, bf16[256,1,128]{0,2,1:T(8,128)(2,1)S(1)}, u32[]{:S(2)}, u32[]{:S(2)}) collective-permute-start(bf16[256,1,128]{0,2,1:T(8,128)(2,1)S(1)} %get-tuple-element.10), channel_id=1, source_target_pairs={{0,16},{4,20},{8,24},{12,28},{16,0},{20,4},{24,8},{28,12},{1,17},{... | collective-permute-start | bytes 196616 | tf_op jit(solution)/shard_map/ppermute | solution.py:22
  18.5 10.6 %collective-permute-start.4 = (bf16[256,1,128]{0,2,1:T(8,128)(2,1)S(1)}, bf16[256,1,128]{0,2,1:T(8,128)(2,1)S(1)}, u32[]{:S(2)}, u32[]{:S(2)}) collective-permute-start(bf16[256,1,128]{0,2,1:T(8,128)(2,1)S(1)} %get-tuple-element.9), channel_id=1, source_target_pairs={{0,12},{4,16},{8,20},{12,24},{16,28},{20,0},{24,4},{28,8},{1,13},{... | collective-permute-start | bytes 196616 | tf_op jit(solution)/shard_map/ppermute | solution.py:22
  18.5 10.6 %collective-permute-start.5 = (bf16[256,1,128]{0,2,1:T(8,128)(2,1)S(1)}, bf16[256,1,128]{0,2,1:T(8,128)(2,1)S(1)}, u32[]{:S(2)}, u32[]{:S(2)}) collective-permute-start(bf16[256,1,128]{0,2,1:T(8,128)(2,1)S(1)} %get-tuple-element.8), channel_id=1, source_target_pairs={{0,8},{4,12},{8,16},{12,20},{16,24},{20,28},{24,0},{28,4},{1,9},{5... | collective-permute-start | bytes 196616 | tf_op jit(solution)/shard_map/ppermute | solution.py:22
  20.4 8.7 %collective-permute-start.6 = (bf16[256,1,128]{0,2,1:T(8,128)(2,1)S(1)}, bf16[256,1,128]{0,2,1:T(8,128)(2,1)S(1)}, u32[]{:S(2)}, u32[]{:S(2)}) collective-permute-start(bf16[256,1,128]{0,2,1:T(8,128)(2,1)S(1)} %get-tuple-element.7), channel_id=1, source_target_pairs={{0,4},{4,8},{8,12},{12,16},{16,20},{20,24},{24,28},{28,0},{1,5},{5... | collective-permute-start | bytes 196616 | tf_op jit(solution)/shard_map/ppermute | solution.py:22
  30.5 10.3 %copy-start.2 = (bf16[128,23,64]{0,2,1:T(8,128)(2,1)S(1)}, bf16[128,23,64]{0,2,1:T(8,128)(2,1)}, u32[]{:S(2)}) copy-start(bf16[128,23,64]{0,2,1:T(8,128)(2,1)} %param.7) | copy-start | bytes 1130500
  40.8 4.8 %copy-start.1 = (bf16[128,8,256]{2,1,0:T(8,128)(2,1)S(1)}, bf16[128,8,256]{2,1,0:T(8,128)(2,1)}, u32[]{:S(2)}) copy-start(bf16[128,8,256]{2,1,0:T(8,128)(2,1)} %param.6) | copy-start | bytes 1572868
  42.1 11.6 %all-to-all-start.1 = ((bf16[128,8,128]{0,2,1:T(8,128)(2,1)}), bf16[128,8,128]{0,2,1:T(8,128)(2,1)S(1)}, u32[]{:S(2)}, u32[]{:S(2)}) async-start(bf16[128,8,128]{0,2,1:T(8,128)(2,1)} %bitcast.14), calls=%async_computation.1 | async-start | bytes 524288 | tf_op jit(solution)/shard_map/all_to_all | solution.py:65
  53.7 17.2 %all-to-all-start = ((bf16[128,8,256]{2,0,1:T(8,128)(2,1)}), bf16[128,8,256]{2,0,1:T(8,128)(2,1)S(1)}, u32[]{:S(2)}, u32[]{:S(2)}) async-start(bf16[128,8,256]{2,0,1:T(8,128)(2,1)} %copy.24), calls=%async_computation | async-start | bytes 1048576 | tf_op jit(solution)/shard_map/all_to_all | solution.py:66
  57.2 73.7 %reduce-scatter.3.cloned.1.call-start = ((), (), s32[]{:S(2)}) async-start(), calls=%async_computation.5 | async-start | bytes 327680 | tf_op jit(solution)/shard_map/reduce_scatter | solution.py:106
  70.9 0.8 copy-start.3
  110.3 1.3 copy-start.4
  111.5 86.7 %reduce-scatter.5.cloned.1.call-start = ((), (), s32[]{:S(2)}) async-start(), calls=%async_computation.6 | async-start | bytes 1695744 | tf_op jit(solution)/shard_map/reduce_scatter | solution.py:118
Sparse Core Ops, SparseCore 0:
  40.9 20.2 all-gather.1
  111.7 19.2 reduce-scatter.2
  134.4 63.7 reduce-scatter.4
